TPU v7x, 32 devices: a whole 2x2x4 slice. The times are simulated.
32 devices in a mesh: seq: 8 (over z, y), mp: 4 (over x, core).
Axes of the slice: x: 2, y: 2, z: 4, core: 2. Of those that a mesh axis runs over, the one named last changes fastest.
Arguments:
- hidden_entry_states: bfloat16 [1024, 512], P('seq'), may hold values from -6 to 6
- base_ids: int32 [1024], P('seq'), may hold values from 0 to 4
- mask_index: int32 [128], P('seq'), may hold values from 0 to 1023, as said below
- first_kernel: bfloat16 [9, 512, 512], P(None, None, 'mp'), may hold values from -0.09375 to 0.09375
- second_kernel: bfloat16 [9, 512, 512], P(None, None, 'mp'), may hold values from -0.09375 to 0.09375
- head_weight: bfloat16 [512, 5], replicated, may hold values from -0.5 to 0.5
Outputs:
- input_grad: bfloat16 [1024, 512], P('seq')
- first_kernel_gradient: float32 [9, 512, 512], P(None, 'seq', 'mp')
- second_kernel_gradient: float32 [9, 512, 512], P(None, 'seq', 'mp')
Inputs may be any that keep to these rules, and one draw needn't show every extreme that they name: `mask_index`: each device's 16 entries are distinct positions within its own block of 128 bases, in no particular order.
All inputs are finite; a program needn't handle non-finite values.
Results may differ from a plain program's by a relative error of at most 0.014.
Values may be sent and summed in bfloat16 or wider, within the bound.
No kernel may reach another device: no remote copies, remote signals or barrier semaphores. Data moves between devices by JAX's collectives and lax.ppermute only.
A program may use at most 64 MiB of HBM per device.

v0:
```python
import jax
import jax.numpy as jnp
from jax import lax
from jax.sharding import PartitionSpec as P

DILATION_FIRST1 = 2048
DILATION_SECOND2 = 4096


epsilon = 1e-05
root_half = 0.7071067811865476
inv_root_two_pi = 0.3989422804014327


def shifted(x, axis, by):
    peers = lax.axis_size(axis)
    pairs = [(i, i + by) for i in range(peers) if 0 <= i + by < peers]
    return lax.ppermute(x, axis, pairs)


def gelu_parts(conv_out):
    normal_cdf = 0.5 * (1.0 + lax.erf(conv_out * root_half))
    gelu_slope = normal_cdf + conv_out * inv_root_two_pi * jnp.exp(-0.5 * conv_out * conv_out)
    return (conv_out * normal_cdf, gelu_slope)


def norm_parts(activation):
    values = activation.astype(jnp.float32)
    centre = jnp.mean(values, axis=-1, keepdims=True)
    centred = values - centre
    spread = jnp.mean(centred * centred, axis=-1, keepdims=True)
    inverse = lax.rsqrt(spread + epsilon)
    return (centred * inverse, inverse)


def loss_grad(hidden_top, targets, head_weight):
    logits = lax.dot_general(
        head_weight, hidden_top, (((0,), (1,)), ((), ())), preferred_element_type=jnp.float32
    )
    exponent = jnp.exp(logits)
    probability = exponent / jnp.sum(exponent, axis=0, keepdims=True)
    vocab_rows = lax.broadcasted_iota(jnp.int32, logits.shape, 0)
    onehot = (vocab_rows == targets[None, :]).astype(jnp.float32)
    weight = (targets >= 0).astype(jnp.float32)[None, :]
    dlogits = weight * (probability - onehot)
    return lax.dot_general(
        dlogits,
        head_weight.astype(jnp.float32),
        (((0,), (1,)), ((), ())),
        precision=lax.Precision.HIGHEST,
    )


def local(hidden_entry_states, base_ids, mask_index, first_kernel, second_kernel, head_weight):
    seq_count = lax.axis_size("seq")
    rows_per_block = hidden_entry_states.shape[0]
    channels = hidden_entry_states.shape[1]
    own_width = first_kernel.shape[2]
    tap_count = first_kernel.shape[0]
    centre_tap = tap_count // 2
    mask_count = mask_index.shape[0]
    device_row = lax.axis_index("seq")
    block_start = device_row * rows_per_block
    offsets = mask_index - block_start
    positions = lax.broadcasted_iota(jnp.int32, (rows_per_block, mask_count), 0)
    masked = jnp.any(positions == offsets[None, :], axis=1)
    targets = jnp.where(masked, base_ids, -1)

    def forward_conv(source, kernel, dilation_blocks):
        pieces = []
        for tap_index in range(tap_count):
            device_hop = dilation_blocks * (tap_index - centre_tap)
            if device_hop == 0:
                pieces.append(source)
            elif abs(device_hop) >= seq_count:
                pieces.append(jnp.zeros_like(source))
            else:
                pieces.append(shifted(source, "seq", -device_hop))
        stacked = jnp.concatenate(pieces, axis=1)
        return jnp.dot(
            stacked,
            kernel.reshape(tap_count * channels, own_width),
            preferred_element_type=jnp.float32,
        )

    def tap_sources(grad_conv, dilation_blocks):
        pieces = []
        for tap_index in range(tap_count):
            device_hop = dilation_blocks * (tap_index - centre_tap)
            if device_hop == 0:
                pieces.append(grad_conv)
            elif abs(device_hop) >= seq_count:
                pieces.append(jnp.zeros_like(grad_conv))
            else:
                pieces.append(shifted(grad_conv, "seq", device_hop))
        return jnp.stack(pieces, axis=0)

    def block_forward_pass(source, kernel, dilation_blocks):
        conv_out = forward_conv(source, kernel, dilation_blocks)
        activation, gelu_slope = gelu_parts(conv_out)
        mixed_all = lax.all_gather(activation.astype(jnp.bfloat16), "mp", axis=1, tiled=True)
        normed, inverse = norm_parts(mixed_all)
        result = (source.astype(jnp.float32) + normed).astype(jnp.bfloat16)
        return (result, (source, normed, inverse, gelu_slope))

    def block_backward_pass(grad_out, saved, kernel, dilation_blocks):
        source, normed, inverse, gelu_slope = saved
        mean_grad = jnp.mean(grad_out, axis=-1, keepdims=True)
        mean_cross = jnp.mean(grad_out * normed, axis=-1, keepdims=True)
        grad_act = inverse * (grad_out - mean_grad - normed * mean_cross)
        own_cols = lax.dynamic_slice_in_dim(
            grad_act, lax.axis_index("mp") * own_width, own_width, 1
        )
        grad_conv = (own_cols * gelu_slope).astype(jnp.bfloat16)
        tap_stack = tap_sources(grad_conv, dilation_blocks)
        input_part = jnp.einsum(
            "kro,kdo->rd", tap_stack, kernel, preferred_element_type=jnp.float32
        )
        grad_in = grad_out + lax.psum(input_part.astype(jnp.bfloat16), "mp").astype(jnp.float32)
        kernel_part = jnp.einsum(
            "rd,kro->kdo", source, tap_stack, preferred_element_type=jnp.float32
        )
        by_owner = kernel_part.reshape(tap_count, seq_count, channels // seq_count, own_width)
        received = lax.all_to_all(
            by_owner.astype(jnp.bfloat16), "seq", split_axis=1, concat_axis=1, tiled=True
        ).astype(by_owner.dtype)
        return (grad_in, jnp.sum(received, axis=1))

    first_receptive_span = DILATION_FIRST1 // rows_per_block
    second_receptive_span = DILATION_SECOND2 // rows_per_block
    hidden_after_first, first_residuals = block_forward_pass(
        hidden_entry_states, first_kernel, first_receptive_span
    )
    hidden_after_second, second_residuals = block_forward_pass(
        hidden_after_first, second_kernel, second_receptive_span
    )
    gradient_after_second = loss_grad(hidden_after_second, targets, head_weight)
    gradient_after_first, second_kernel_gradient = block_backward_pass(
        gradient_after_second, second_residuals, second_kernel, second_receptive_span
    )
    gradient_before_first, first_kernel_gradient = block_backward_pass(
        gradient_after_first, first_residuals, first_kernel, first_receptive_span
    )
    input_grad = gradient_before_first.astype(jnp.bfloat16)
    return (input_grad, first_kernel_gradient, second_kernel_gradient)


def solution(mesh):
    placed = (P("seq", None), P("seq"), P("seq"), P(None, None, "mp"), P(None, None, "mp"), P())
    return jax.shard_map(
        local,
        mesh=mesh,
        in_specs=placed,
        out_specs=(P("seq", None), P(None, "seq", "mp"), P(None, "seq", "mp")),
        check_vma=False,
    )
```

profile of v0, /device:TPU:0, one launch (start us, length us, event | category | flops | bytes accessed | tf_op | source)
XLA Modules:
  0.0 132.1 jit_solution(16882621267239192287)
XLA Ops:
  7.2 0.8 broadcast_subtract_fusion
  8.1 2.5 %multiply_convert_fusion.1 = (bf16[128,128]{1,0:T(8,128)(2,1)S(1)}, f32[128,128]{1,0:T(8,128)}) fusion(bf16[4608,128]{1,0:T(8,128)(2,1)} %bitcast.42, bf16[128,2048]{1,0:T(8,128)(2,1)S(1)} %broadcast.90, bf16[128,512]{1,0:T(8,128)(2,1)} %param.6), kind=kOutput, calls=%fused_computation.63 | convolution fusion | flops 154615808 | bytes 1933312 | tf_op jit(solution)/shard_map/dot_general | solution.py:80
  10.6 6.5 %all_gather.6 = bf16[128,512]{1,0:T(8,128)(2,1)S(1)} all-gather(bf16[128,128]{1,0:T(8,128)(2,1)S(1)} %get-tuple-element.13), channel_id=1, replica_groups=mesh['seq'=8,'mp'=4] {'mp'}, dimensions={1}, use_global_device_ids=true | all-gather | bytes 163840 | tf_op jit(solution)/shard_map/all_gather | solution.py:101
  17.7 0.8 fusion.8
  19.1 5.6 %all_gather.7 = bf16[128,512]{1,0:T(8,128)(2,1)S(1)} all-gather(bf16[128,128]{1,0:T(8,128)(2,1)S(1)} %get-tuple-element.15), channel_id=1, replica_groups=mesh['seq'=8,'mp'=4] {'mp'}, dimensions={1}, use_global_device_ids=true | all-gather | bytes 163840 | tf_op jit(solution)/shard_map/all_gather | solution.py:101
  27.0 0.6 copy-done.6
  28.2 0.7 copy.25
  28.9 1.1 copy.26
  30.0 6.2 %all-to-all-start.1 = ((bf16[9,8,64,128]{3,2,0,1:T(8,128)(2,1)}), bf16[9,8,64,128]{3,2,0,1:T(8,128)(2,1)S(1)}, u32[]{:S(2)}, u32[]{:S(2)}) async-start(bf16[9,8,64,128]{3,2,0,1:T(8,128)(2,1)} %copy.26), calls=%async_computation.1 | async-start | bytes 2359296 | tf_op jit(solution)/shard_map/all_to_all | solution.py:124
  36.3 1.2 fusion.6
  37.5 35.1 %all-reduce.3.cloned.1.call-done = bf16[128,512]{1,0:T(8,128)(2,1)} async-done(((bf16[128,512]{1,0:T(8,128)(2,1)}), bf16[128,512]{1,0:T(8,128)(2,1)}) %all-reduce.3.cloned.1.call-update) | async-done | bytes 131088 | tf_op jit(solution)/shard_map/psum | solution.py:119
  72.6 1.1 fusion.48
  73.7 0.7 copy-done.5
  74.4 1.0 fusion.30
  75.3 0.6 copy-done.10
  75.9 1.5 %fusion = bf16[9,512,128]{1,2,0:T(8,128)(2,1)} fusion(bf16[4,128,128]{2,1,0:T(8,128)(2,1)S(1)} %copy-done.7, bf16[1,128,128]{2,1,0:T(8,128)(2,1)S(1)} %fusion.30, bf16[128,512]{1,0:T(8,128)(2,1)S(1)} %copy-done.9), kind=kOutput, calls=%fused_computation.8 | convolution fusion | flops 151879680 | bytes 1474560 | tf_op jit(solution)/shard_map/rd,kro->kdo/dot_general | solution.py:120
  77.5 1.7 %copy.22 = bf16[9,512,128]{2,1,0:T(8,128)(2,1)S(1)} copy(bf16[9,512,128]{1,2,0:T(8,128)(2,1)} %fusion) | data formatting | bytes 2359296 | tf_op jit(solution)/shard_map/convert_element_type | solution.py:125
  79.2 1.1 copy.23
  80.3 5.5 %all-to-all-start = ((bf16[9,8,64,128]{3,2,0,1:T(8,128)(2,1)}), bf16[9,8,64,128]{3,2,0,1:T(8,128)(2,1)S(1)}, u32[]{:S(2)}, u32[]{:S(2)}) async-start(bf16[9,8,64,128]{3,2,0,1:T(8,128)(2,1)} %copy.23), calls=%async_computation | async-start | bytes 2359296 | tf_op jit(solution)/shard_map/all_to_all | solution.py:124
  85.9 2.6 %fusion.7 = bf16[128,512]{1,0:T(8,128)(2,1)} fusion(bf16[9,512,128]{2,1,0:T(8,128)(2,1)} %param.9, bf16[4,128,128]{2,1,0:T(8,128)(2,1)} %copy-done.6, bf16[1,128,128]{2,1,0:T(8,128)(2,1)} %copy-done.10), kind=kOutput, calls=%fused_computation.17 | convolution fusion | flops 151355392 | bytes 1474560 | tf_op jit(solution)/shard_map/kro,kdo->rd/dot_general | solution.py:116
  88.5 33.3 %all-reduce.5.cloned.1.call-done = bf16[128,512]{1,0:T(8,128)(2,1)} async-done(((bf16[128,512]{1,0:T(8,128)(2,1)}), bf16[128,512]{1,0:T(8,128)(2,1)}) %all-reduce.5.cloned.1.call-update) | async-done | bytes 131088 | tf_op jit(solution)/shard_map/psum | solution.py:119
  121.8 1.7 %add_convert_fusion = bf16[128,512]{1,0:T(8,128)(2,1)} fusion(f32[128,512]{1,0:T(8,128)} %copy-done.5, bf16[128,512]{1,0:T(8,128)(2,1)} %all-reduce.5.cloned.1.call-done), kind=kLoop, calls=%fused_computation.33 | loop fusion | flops 196608 | bytes 524288 | tf_op jit(solution)/shard_map/convert_element_type | solution.py:144
  123.5 0.9 convert_reduce_fusion
  124.4 0.9 convert_reduce_fusion.1
  (55 shorter events, 4.2 us)
Async XLA Ops:
  7.2 11.4 %copy-start = (bf16[9,512,128]{2,1,0:T(8,128)(2,1)S(1)}, bf16[9,512,128]{2,1,0:T(8,128)(2,1)}, u32[]{:S(2)}) copy-start(bf16[9,512,128]{2,1,0:T(8,128)(2,1)} %param.10) | copy-start | bytes 3538948
  8.1 9.7 %copy-start.8 = (bf16[128,512]{1,0:T(8,128)(2,1)S(1)}, bf16[128,512]{1,0:T(8,128)(2,1)}, u32[]{:S(2)}) copy-start(bf16[128,512]{1,0:T(8,128)(2,1)} %param.6) | copy-start | bytes 393220
  17.1 0.7 copy-start.1
  18.6 6.4 %copy-start.15 = (s32[128]{0:T(128)S(1)}, s32[128]{0:T(128)}, u32[]{:S(2)}) copy-start(s32[128]{0:T(128)} %param.7) | copy-start | bytes 1540
  18.6 6.4 %copy-start.14 = (bf16[512,5]{0,1:T(8,128)(2,1)S(1)}, bf16[512,5]{0,1:T(8,128)(2,1)}, u32[]{:S(2)}) copy-start(bf16[512,5]{0,1:T(8,128)(2,1)} %param.11) | copy-start | bytes 15364
  25.7 0.7 copy-start.3
  26.4 0.6 copy-start.11
  27.0 0.6 copy-start.6
  30.0 6.3 %copy-start.7 = (bf16[4,128,128]{2,1,0:T(8,128)(2,1)S(1)}, bf16[4,128,128]{2,1,0:T(8,128)(2,1)}, u32[]{:S(2)}) copy-start(bf16[4,128,128]{2,1,0:T(8,128)(2,1)} %copy-done.6) | copy-start | bytes 393220
  30.0 6.3 %copy-start.12 = (bf16[1,128,128]{2,1,0:T(8,128)(2,1)S(1)}, bf16[1,128,128]{2,1,0:T(8,128)(2,1)}, u32[]{:S(2)}) copy-start(bf16[1,128,128]{2,1,0:T(8,128)(2,1)} %copy-done.11) | copy-start | bytes 98308
  30.0 50.3 %all-to-all-start.1 = ((bf16[9,8,64,128]{3,2,0,1:T(8,128)(2,1)}), bf16[9,8,64,128]{3,2,0,1:T(8,128)(2,1)S(1)}, u32[]{:S(2)}, u32[]{:S(2)}) async-start(bf16[9,8,64,128]{3,2,0,1:T(8,128)(2,1)} %copy.26), calls=%async_computation.1 | async-start | bytes 2359296 | tf_op jit(solution)/shard_map/all_to_all | solution.py:124
  36.2 36.4 %copy-start.2 = (bf16[128,512]{1,0:T(8,128)(2,1)S(1)}, bf16[128,512]{1,0:T(8,128)(2,1)}, u32[]{:S(2)}) copy-start(bf16[128,512]{1,0:T(8,128)(2,1)} %copy-done.1) | copy-start | bytes 393220
  36.2 36.4 %copy-start.4 = (f32[128,512]{1,0:T(8,128)S(1)}, f32[128,512]{1,0:T(8,128)}, u32[]{:S(2)}) copy-start(f32[128,512]{1,0:T(8,128)} %copy-done.3) | copy-start | bytes 786436
  36.2 38.2 %copy-start.13 = (f32[128,128]{1,0:T(8,128)S(1)}, f32[128,128]{1,0:T(8,128)}, u32[]{:S(2)}) copy-start(f32[128,128]{1,0:T(8,128)} %get-tuple-element.14) | copy-start | bytes 196612
  36.2 39.7 %copy-start.9 = (bf16[128,512]{1,0:T(8,128)(2,1)S(1)}, bf16[128,512]{1,0:T(8,128)(2,1)}, u32[]{:S(2)}) copy-start(bf16[128,512]{1,0:T(8,128)(2,1)} %param.6) | copy-start | bytes 393220
  36.2 36.3 %all-reduce.3.cloned.1.call-start = ((), (), s32[]{:S(2)}) async-start(), calls=%async_computation.2 | async-start | bytes 262144 | tf_op jit(solution)/shard_map/psum | solution.py:119
  73.6 0.7 copy-start.5
  75.3 0.6 copy-start.10
  80.3 44.1 %all-to-all-start = ((bf16[9,8,64,128]{3,2,0,1:T(8,128)(2,1)}), bf16[9,8,64,128]{3,2,0,1:T(8,128)(2,1)S(1)}, u32[]{:S(2)}, u32[]{:S(2)}) async-start(bf16[9,8,64,128]{3,2,0,1:T(8,128)(2,1)} %copy.23), calls=%async_computation | async-start | bytes 2359296 | tf_op jit(solution)/shard_map/all_to_all | solution.py:124
  85.8 36.0 %all-reduce.5.cloned.1.call-start = ((), (), s32[]{:S(2)}) async-start(), calls=%async_computation.3 | async-start | bytes 262144 | tf_op jit(solution)/shard_map/psum | solution.py:119
Sparse Core Ops, SparseCore 0:
  39.3 33.1 all-reduce.2
  89.5 32.2 all-reduce.4
where the time goes:
time: 133 us; the launch traced here: 132 us
  waiting for transfers between devices  68.4 us (51%)
  between operations  14.3 us (11%)
  blocking collectives  12.1 us (9%)
  starting transfers between devices  11.8 us (9%)
  matrix products  9.42 us (7%)
  local copies, waits for them, and re-layouts  8.16 us (6%)
  other arithmetic  7.94 us (6%)
    psum x2, waiting for transfers between devices, block_backward_pass(): lax.psum(input_part.astype(jnp.bfloat16), 'mp').astype(jnp.float32)  68.4 us
    all_gather x2, blocking collectives, block_forward_pass(): lax.all_gather(activation.astype(jnp.bfloat16), 'mp', axis=1, tiled=True)  12.1 us
    all_to_all x2, starting transfers between devices, block_backward_pass(): lax.all_to_all(by_owner.astype(jnp.bfloat16), 'seq', split_axis=1, concat...  11.7 us
    convert_element_type x4, local copies, waits for them, and re-layouts, block_backward_pass(): by_owner.astype(jnp.bfloat16)  4.65 us
    dot_general x2, matrix products, block_backward_pass(): jnp.einsum('kro,kdo->rd', tap_stack, kernel, preferred_element_type=jnp.f...  3.77 us
    unnamed x32, local copies, waits for them, and re-layouts  3.45 us
    dot_general x2, matrix products, forward_conv(): jnp.dot(stacked, kernel.reshape(tap_count * channels, own_width), preferr...  2.92 us
  transfers between devices with their start and end apart: 4, of which 2 were waited for; matrix products, arithmetic and copies ran while one was open for 10% of the time, Pallas kernels for 0%

commit v1 on v0

v1 whole, which is shorter than its diff:
```python
import jax
import jax.numpy as jnp
from jax import lax
from jax.experimental import pallas as pl
from jax.experimental.pallas import tpu as pltpu
from jax.sharding import PartitionSpec as P

DILATION_FIRST1 = 2048
DILATION_SECOND2 = 4096


epsilon = 1e-05
root_half = 0.7071067811865476
inv_root_two_pi = 0.3989422804014327
ROW_CHUNK = 32


def gelu_parts(conv_out):
    normal_cdf = 0.5 * (1.0 + lax.erf(conv_out * root_half))
    gelu_slope = normal_cdf + conv_out * inv_root_two_pi * jnp.exp(-0.5 * conv_out * conv_out)
    return (conv_out * normal_cdf, gelu_slope)


def norm_parts(activation):
    values = activation.astype(jnp.float32)
    centre = jnp.mean(values, axis=-1, keepdims=True)
    centred = values - centre
    spread = jnp.mean(centred * centred, axis=-1, keepdims=True)
    inverse = lax.rsqrt(spread + epsilon)
    return (centred * inverse, inverse)


def active_hops(tap_count, dilation_blocks, seq_count):
    centre_tap = tap_count // 2
    hops = [(tap, dilation_blocks * (tap - centre_tap)) for tap in range(tap_count)]
    return [(tap, hop) for tap, hop in hops if abs(hop) < seq_count]


def shifted(x, axis, by):
    if by == 0:
        return x
    peers = lax.axis_size(axis)
    pairs = [(i, i + by) for i in range(peers) if 0 <= i + by < peers]
    return lax.ppermute(x, axis, pairs)


def loss_grad(hidden_top, targets, head_weight):
    logits = lax.dot_general(
        head_weight, hidden_top, (((0,), (1,)), ((), ())), preferred_element_type=jnp.float32
    )
    exponent = jnp.exp(logits)
    probability = exponent / jnp.sum(exponent, axis=0, keepdims=True)
    vocab_rows = lax.broadcasted_iota(jnp.int32, logits.shape, 0)
    onehot = (vocab_rows == targets[None, :]).astype(jnp.float32)
    weight = (targets >= 0).astype(jnp.float32)[None, :]
    dlogits = weight * (probability - onehot)
    return lax.dot_general(
        dlogits,
        head_weight.astype(jnp.float32),
        (((0,), (1,)), ((), ())),
        precision=lax.Precision.HIGHEST,
    )


def general_plan(hidden_entry_states, base_ids, mask_index, first_kernel, second_kernel, head_weight, first_hops, second_hops):
    seq_count = lax.axis_size("seq")
    rows_per_block, channels = hidden_entry_states.shape
    tap_count, _, own_width = first_kernel.shape
    mask_count = mask_index.shape[0]
    offsets = mask_index - lax.axis_index("seq") * rows_per_block
    positions = lax.broadcasted_iota(jnp.int32, (rows_per_block, mask_count), 0)
    masked = jnp.any(positions == offsets[None, :], axis=1)
    targets = jnp.where(masked, base_ids, -1)

    def used(kernel, hops):
        first_tap, last_tap = hops[0][0], hops[-1][0]
        return kernel[first_tap : last_tap + 1]

    def block_forward_pass(source, kernel, hops):
        stacked = jnp.concatenate([shifted(source, "seq", -hop) for _, hop in hops], axis=1)
        conv_out = jnp.dot(
            stacked,
            used(kernel, hops).reshape(len(hops) * channels, own_width),
            preferred_element_type=jnp.float32,
        )
        activation, gelu_slope = gelu_parts(conv_out)
        mixed_all = lax.all_gather(activation.astype(jnp.bfloat16), "mp", axis=1, tiled=True)
        normed, inverse = norm_parts(mixed_all)
        result = (source.astype(jnp.float32) + normed).astype(jnp.bfloat16)
        return (result, (source, normed, inverse, gelu_slope))

    def block_backward_pass(grad_out, saved, kernel, hops):
        source, normed, inverse, gelu_slope = saved
        mean_grad = jnp.mean(grad_out, axis=-1, keepdims=True)
        mean_cross = jnp.mean(grad_out * normed, axis=-1, keepdims=True)
        grad_act = inverse * (grad_out - mean_grad - normed * mean_cross)
        own_cols = lax.dynamic_slice_in_dim(
            grad_act, lax.axis_index("mp") * own_width, own_width, 1
        )
        grad_conv = (own_cols * gelu_slope).astype(jnp.bfloat16)
        tap_stack = jnp.stack([shifted(grad_conv, "seq", hop) for _, hop in hops], axis=0)
        input_part = jnp.einsum(
            "kro,kdo->rd", tap_stack, used(kernel, hops), preferred_element_type=jnp.float32
        )
        grad_in = grad_out + lax.psum(input_part.astype(jnp.bfloat16), "mp").astype(jnp.float32)
        kernel_part = jnp.einsum(
            "rd,kro->kdo", source, tap_stack, preferred_element_type=jnp.float32
        )
        by_owner = kernel_part.reshape(len(hops), seq_count, channels // seq_count, own_width)
        received = lax.all_to_all(
            by_owner.astype(jnp.bfloat16), "seq", split_axis=1, concat_axis=1, tiled=True
        ).astype(by_owner.dtype)
        first_tap, last_tap = hops[0][0], hops[-1][0]
        kernel_grad = jnp.pad(
            jnp.sum(received, axis=1),
            ((first_tap, tap_count - 1 - last_tap), (0, 0), (0, 0)),
        )
        return (grad_in, kernel_grad)

    hidden_one, saved_one = block_forward_pass(hidden_entry_states, first_kernel, first_hops)
    hidden_two, saved_two = block_forward_pass(hidden_one, second_kernel, second_hops)
    grad_two = loss_grad(hidden_two, targets, head_weight)
    grad_one, second_grad = block_backward_pass(grad_two, saved_two, second_kernel, second_hops)
    grad_zero, first_grad = block_backward_pass(grad_one, saved_one, first_kernel, first_hops)
    return (grad_zero.astype(jnp.bfloat16), first_grad, second_grad)


NT = (((1,), (1,)), ((), ()))
TN = (((0,), (0,)), ((), ()))


def dot(a, b, dims=(((1,), (0,)), ((), ()))):
    return lax.dot_general(a, b, dims, preferred_element_type=jnp.float32)


def column_block(me, offset, width):
    return pl.ds(pl.multiple_of((me ^ offset) * width, width), width)


def gather_by_offset(own, count):
    blocks = {0: own}
    bit = count // 2
    while bit:
        pairs = [(i, i ^ bit) for i in range(count)]
        for offset in list(blocks):
            blocks[offset ^ bit] = lax.ppermute(blocks[offset], "mp", pairs)
        bit //= 2
    return [blocks[offset] for offset in range(count)]


def chunks(rows):
    size = ROW_CHUNK if rows % ROW_CHUNK == 0 else rows
    return [pl.ds(start, size) for start in range(0, rows, size)]


def norm_backward(grad_out, normed, inverse, gelu_slope):
    mean_grad = jnp.mean(grad_out, axis=-1, keepdims=True)
    mean_cross = jnp.mean(grad_out * normed, axis=-1, keepdims=True)
    grad_act = inverse * (grad_out - mean_grad - normed * mean_cross)
    return (grad_act * gelu_slope).astype(jnp.bfloat16)


def block_forward(me, source_ref, kernel_refs, conv_ref, hidden_ref, normed_ref, inverse_ref, slope_ref):
    width = kernel_refs[0].shape[1]
    source = source_ref[...]
    for offset, kernel_ref in enumerate(kernel_refs):
        conv_ref[:, column_block(me, offset, width)] = dot(source, kernel_ref[...])
    for rows in chunks(source_ref.shape[0]):
        activation, gelu_slope = gelu_parts(conv_ref[rows, :])
        normed, inverse = norm_parts(activation.astype(jnp.bfloat16))
        slope_ref[rows, :] = gelu_slope
        normed_ref[rows, :] = normed
        inverse_ref[rows, :] = inverse
        hidden_ref[rows, :] = (source_ref[rows, :].astype(jnp.float32) + normed).astype(jnp.bfloat16)


def first_block_body(count, me_ref, source_ref, *refs):
    kernel_refs = refs[:count]
    hidden_ref, normed_ref, inverse_ref, slope_ref, conv_ref = refs[count:]
    block_forward(me_ref[0], source_ref, kernel_refs, conv_ref, hidden_ref, normed_ref, inverse_ref, slope_ref)


def kernel_part(source_ref, grad_conv_ref, me, part_ref, slot):
    width = part_ref.shape[3]
    own = grad_conv_ref[:, column_block(me, 0, width)]
    part = dot(source_ref[...], own, TN).astype(jnp.bfloat16)
    depth = part_ref.shape[2]
    for owner in range(part_ref.shape[0]):
        part_ref[owner, slot] = part[owner * depth : (owner + 1) * depth]


def input_part(grad_conv_ref, kernel_refs, me):
    width = kernel_refs[0].shape[1]
    total = None
    for offset, kernel_ref in enumerate(kernel_refs):
        term = dot(grad_conv_ref[:, column_block(me, offset, width)], kernel_ref[...], NT)
        total = term if total is None else total + term
    return total


def rest_body(count, me_ref, mask_ref, source_ref, hidden_one_ref, normed_one_ref, inverse_one_ref, slope_one_ref, ids_ref, head_ref, *refs):
    first_refs = refs[:count]
    second_refs = refs[count : 2 * count]
    input_grad_ref, part_ref = refs[2 * count : 2 * count + 2]
    conv_ref, hidden_two_ref, normed_two_ref, inverse_two_ref, slope_two_ref, grad_ref, grad_conv_ref = refs[2 * count + 2 :]
    me = me_ref[0]
    block_forward(me, hidden_one_ref, second_refs, conv_ref, hidden_two_ref, normed_two_ref, inverse_two_ref, slope_two_ref)

    head = head_ref[...]
    logits = dot(head, hidden_two_ref[...], NT)
    exponent = jnp.exp(logits)
    probability = exponent / jnp.sum(exponent, axis=0, keepdims=True)
    onehot = (lax.broadcasted_iota(jnp.int32, logits.shape, 0) == ids_ref[...]).astype(jnp.float32)
    positions = lax.broadcasted_iota(jnp.int32, ids_ref.shape, 1) + me_ref[1]
    weight = jnp.zeros(ids_ref.shape, jnp.float32)
    for entry in range(mask_ref.shape[0]):
        weight = jnp.where(positions == mask_ref[entry], 1.0, weight)
    grad_logits = weight * (probability - onehot)
    grad_ref[...] = lax.dot_general(
        grad_logits,
        head.astype(jnp.float32),
        TN,
        precision=lax.Precision.HIGHEST,
        preferred_element_type=jnp.float32,
    )

    all_rows = chunks(source_ref.shape[0])
    for rows in all_rows:
        grad_conv_ref[rows, :] = norm_backward(
            grad_ref[rows, :], normed_two_ref[rows, :], inverse_two_ref[rows, :], slope_two_ref[rows, :]
        )
    kernel_part(hidden_one_ref, grad_conv_ref, me, part_ref, 1)
    grad_ref[...] += input_part(grad_conv_ref, second_refs, me)
    for rows in all_rows:
        grad_conv_ref[rows, :] = norm_backward(
            grad_ref[rows, :], normed_one_ref[rows, :], inverse_one_ref[rows, :], slope_one_ref[rows, :]
        )
    kernel_part(source_ref, grad_conv_ref, me, part_ref, 0)
    input_grad_ref[...] = (grad_ref[...] + input_part(grad_conv_ref, first_refs, me)).astype(jnp.bfloat16)


def local_plan(hidden_entry_states, base_ids, mask_index, first_kernel, second_kernel, head_weight):
    seq_count = lax.axis_size("seq")
    mp_count = lax.axis_size("mp")
    rows, channels = hidden_entry_states.shape
    tap_count, _, own_width = first_kernel.shape
    centre_tap = tap_count // 2
    me = lax.axis_index("mp")
    where = jnp.stack([me, lax.axis_index("seq") * rows]).astype(jnp.int32)
    first = gather_by_offset(first_kernel[centre_tap], mp_count)
    second = gather_by_offset(second_kernel[centre_tap], mp_count)

    vmem = pl.BlockSpec(memory_space=pltpu.VMEM)
    smem = pl.BlockSpec(memory_space=pltpu.SMEM)
    wide = jax.ShapeDtypeStruct((rows, channels), jnp.float32)
    thin = jax.ShapeDtypeStruct((rows, 1), jnp.float32)
    half = jax.ShapeDtypeStruct((rows, channels), jnp.bfloat16)
    params = pltpu.CompilerParams(vmem_limit_bytes=16 * 1024 * 1024)
    hidden_one, normed_one, inverse_one, slope_one = pl.pallas_call(
        lambda *refs: first_block_body(mp_count, *refs),
        out_shape=(half, wide, thin, wide),
        in_specs=[smem] + [vmem] * (1 + mp_count),
        out_specs=(vmem,) * 4,
        scratch_shapes=[pltpu.VMEM((rows, channels), jnp.float32)],
        compiler_params=params,
        name="first_block",
    )(where, hidden_entry_states, *first)

    part_shape = jax.ShapeDtypeStruct((seq_count, 2, channels // seq_count, own_width), jnp.bfloat16)
    input_grad, parts = pl.pallas_call(
        lambda *refs: rest_body(mp_count, *refs),
        out_shape=(half, part_shape),
        in_specs=[smem, smem] + [vmem] * (7 + 2 * mp_count),
        out_specs=(vmem, vmem),
        scratch_shapes=[
            pltpu.VMEM((rows, channels), jnp.float32),
            pltpu.VMEM((rows, channels), jnp.bfloat16),
            pltpu.VMEM((rows, channels), jnp.float32),
            pltpu.VMEM((rows, 1), jnp.float32),
            pltpu.VMEM((rows, channels), jnp.float32),
            pltpu.VMEM((rows, channels), jnp.float32),
            pltpu.VMEM((rows, channels), jnp.bfloat16),
        ],
        compiler_params=params,
        name="rest",
    )(
        where,
        mask_index,
        hidden_entry_states,
        hidden_one,
        normed_one,
        inverse_one,
        slope_one,
        base_ids[None, :],
        head_weight.T,
        *first,
        *second,
    )
    received = lax.all_to_all(parts, "seq", split_axis=0, concat_axis=0, tiled=True)
    totals = jnp.sum(received.astype(jnp.float32), axis=0)
    edges = ((centre_tap, tap_count - 1 - centre_tap), (0, 0), (0, 0))
    return (input_grad, jnp.pad(totals[0:1], edges), jnp.pad(totals[1:2], edges))


def local(hidden_entry_states, base_ids, mask_index, first_kernel, second_kernel, head_weight):
    rows = hidden_entry_states.shape[0]
    tap_count = first_kernel.shape[0]
    seq_count = lax.axis_size("seq")
    mp_count = lax.axis_size("mp")
    first_hops = active_hops(tap_count, DILATION_FIRST1 // rows, seq_count)
    second_hops = active_hops(tap_count, DILATION_SECOND2 // rows, seq_count)
    args = (hidden_entry_states, base_ids, mask_index, first_kernel, second_kernel, head_weight)
    if len(first_hops) == 1 and len(second_hops) == 1 and mp_count & (mp_count - 1) == 0:
        return local_plan(*args)
    return general_plan(*args, first_hops, second_hops)


def solution(mesh):
    placed = (P("seq", None), P("seq"), P("seq"), P(None, None, "mp"), P(None, None, "mp"), P())
    return jax.shard_map(
        local,
        mesh=mesh,
        in_specs=placed,
        out_specs=(P("seq", None), P(None, "seq", "mp"), P(None, "seq", "mp")),
        check_vma=False,
    )
```

time: 133 us -> 33.8 us (0.25)
  waiting for transfers between devices: 68.4 us -> 4.73 us
  between operations: 14.3 us -> 0.74 us
  matrix products: 9.42 us -> 0 us
  starting transfers between devices: 11.8 us -> 3.69 us
  other arithmetic: 7.94 us -> 0.11 us
  Pallas kernels: 0 us -> 4.57 us
  local copies, waits for them, and re-layouts: 8.16 us -> 4.24 us
  blocking collectives: 12.1 us -> 15.5 us
    psum x2 -> x0, waiting for transfers between devices: 68.4 us -> none  [block_backward_pass(): lax.psum(input_part.astype(jnp.bfloat16), 'mp').astype(jnp.float32)]
    all_to_all x0 -> x1, blocking collectives: none -> 15.5 us  [local_plan(): lax.all_to_all(parts, 'seq', split_axis=0, concat_axis=0, tiled=True)]
    all_gather x2 -> x0, blocking collectives: 12.1 us -> none  [block_forward_pass(): lax.all_gather(activation.astype(jnp.bfloat16), 'mp', axis=1, tiled=True)]
    all_to_all x2 -> x0, starting transfers between devices: 11.7 us -> none  [block_backward_pass(): lax.all_to_all(by_owner.astype(jnp.bfloat16), 'seq', split_axis=1, concat...]
    dot_general x8 -> x0, matrix products: 9.42 us -> none  [the longest x2 3.77 us: block_backward_pass(): jnp.einsum('kro,kdo->rd', tap_stack, kernel, preferred_element_type=jnp.f...]
    ppermute x0 -> x6, waiting for transfers between devices: none -> 4.73 us  [gather_by_offset(): blocks[offset ^ bit] = lax.ppermute(blocks[offset], 'mp', pairs)]
    convert_element_type x4 -> x0, local copies, waits for them, and re-layouts: 4.65 us -> none  [block_backward_pass(): by_owner.astype(jnp.bfloat16)]
    pallas_call x0 -> x2, Pallas kernels: none -> 4.57 us  [the longest x1 3.45 us: local_plan(): pl.pallas_call(lambda *refs: rest_body(mp_count, *refs), out_shape=(half,...]
  transfers between devices with their start and end apart: 4 -> 6, of which waited for: 2 -> 2; matrix products, arithmetic and copies ran while one was open for 10% -> 3% of each run, Pallas kernels for 0% -> 3%
where the time goes in v1:
time: 33.8 us; the launch traced here: 33.5 us
  blocking collectives  15.5 us (46%)
  waiting for transfers between devices  4.73 us (14%)
  Pallas kernels  4.57 us (14%)
  local copies, waits for them, and re-layouts  4.24 us (13%)
  starting transfers between devices  3.69 us (11%)
  between operations  0.74 us (2%)
    all_to_all x1, blocking collectives, local_plan(): lax.all_to_all(parts, 'seq', split_axis=0, concat_axis=0, tiled=True)  15.5 us
    ppermute x6, waiting for transfers between devices, gather_by_offset(): blocks[offset ^ bit] = lax.ppermute(blocks[offset], 'mp', pairs)  4.73 us
    ppermute x6, starting transfers between devices, gather_by_offset(): blocks[offset ^ bit] = lax.ppermute(blocks[offset], 'mp', pairs)  3.69 us
    pallas_call x1, Pallas kernels, local_plan(): pl.pallas_call(lambda *refs: rest_body(mp_count, *refs), out_shape=(half,...  3.45 us
    pallas_call x1, Pallas kernels, local_plan(): pl.pallas_call(lambda *refs: first_block_body(mp_count, *refs), out_shape...  1.12 us
    squeeze x1, local copies, waits for them, and re-layouts, local_plan(): first = gather_by_offset(first_kernel[centre_tap], mp_count)  0.93 us
    unnamed x8, local copies, waits for them, and re-layouts  0.92 us
    squeeze x1, local copies, waits for them, and re-layouts, local_plan(): second = gather_by_offset(second_kernel[centre_tap], mp_count)  0.91 us
  transfers between devices with their start and end apart: 6, of which 2 were waited for; matrix products, arithmetic and copies ran while one was open for 3% of the time, Pallas kernels for 3%

profile of v1, /device:TPU:0, one launch (start us, length us, event | category | flops | bytes accessed | tf_op | source)
XLA Modules:
  0.0 33.5 jit_solution(9947848015402092223)
XLA Ops:
  0.6 0.0 copy-start.1
  0.6 0.0 copy-start.2
  0.7 0.0 copy-start.3
  0.7 0.9 %slice_bitcast_fusion.1.refs_2_.refs_9_ = bf16[512,128]{1,0:T(8,128)(2,1)S(1)} fusion(bf16[9,512,128]{2,1,0:T(8,128)(2,1)} %param.9), kind=kLoop, calls=%fused_computation.2 | loop fusion | bytes 262144 | tf_op jit(solution)/shard_map/squeeze | solution.py:250
  1.6 3.0 %collective-permute-start.1 = (bf16[512,128]{1,0:T(8,128)(2,1)S(1)}, bf16[512,128]{1,0:T(8,128)(2,1)S(1)}, u32[]{:S(2)}, u32[]{:S(2)}) collective-permute-start(bf16[512,128]{1,0:T(8,128)(2,1)S(1)} %slice_bitcast_fusion.1.refs_2_.refs_9_), channel_id=1, source_target_pairs={{0,2},{1,3},{2,0},{3,1},{4,6},{5,7},{6,4},{7,5},{8,10},{9,11},{10,... | collective-permute-start | bytes 393224 | tf_op jit(solution)/shard_map/ppermute | solution.py:146
  4.6 0.9 %slice_bitcast_fusion.refs_13_ = bf16[512,128]{1,0:T(8,128)(2,1)S(1)} fusion(bf16[9,512,128]{2,1,0:T(8,128)(2,1)} %param.10), kind=kLoop, calls=%fused_computation.1 | loop fusion | bytes 262144 | tf_op jit(solution)/shard_map/squeeze | solution.py:251
  5.5 0.1 collective-permute-start.4
  5.6 0.1 collective-permute-start
  5.7 2.8 %collective-permute-done.1.refs_4_.refs_11_ = bf16[512,128]{1,0:T(8,128)(2,1)S(1)} collective-permute-done((bf16[512,128]{1,0:T(8,128)(2,1)S(1)}, bf16[512,128]{1,0:T(8,128)(2,1)S(1)}, u32[]{:S(2)}, u32[]{:S(2)}) %collective-permute-start.1) | collective-permute-done | bytes 131104 | tf_op jit(solution)/shard_map/ppermute | solution.py:146
  8.5 0.0 collective-permute-start.2
  8.5 0.5 %collective-permute-start.3 = (bf16[512,128]{1,0:T(8,128)(2,1)S(1)}, bf16[512,128]{1,0:T(8,128)(2,1)S(1)}, u32[]{:S(2)}, u32[]{:S(2)}) collective-permute-start(bf16[512,128]{1,0:T(8,128)(2,1)S(1)} %slice_bitcast_fusion.refs_13_), channel_id=1, source_target_pairs={{0,1},{1,0},{2,3},{3,2},{4,5},{5,4},{6,7},{7,6},{8,9},{9,8},{10,11... | collective-permute-start | bytes 393224 | tf_op jit(solution)/shard_map/ppermute | solution.py:146
  9.0 1.9 %collective-permute-done.4.refs_15_ = bf16[512,128]{1,0:T(8,128)(2,1)S(1)} collective-permute-done((bf16[512,128]{1,0:T(8,128)(2,1)S(1)}, bf16[512,128]{1,0:T(8,128)(2,1)S(1)}, u32[]{:S(2)}, u32[]{:S(2)}) %collective-permute-start.4) | collective-permute-done | bytes 131104 | tf_op jit(solution)/shard_map/ppermute | solution.py:146
  10.9 0.0 collective-permute-start.5
  10.9 0.1 pad_add_fusion.refs_0_
  11.0 0.0 collective-permute-done.refs_3_.refs_10_
  11.0 0.0 collective-permute-done.2.refs_5_.refs_12_
  11.0 0.9 %copy-done = bf16[128,512]{1,0:T(8,128)(2,1)S(1)} copy-done((bf16[128,512]{1,0:T(8,128)(2,1)S(1)}, bf16[128,512]{1,0:T(8,128)(2,1)}, u32[]{:S(2)}) %copy-start) | copy-done | bytes 131096
  11.9 1.1 %first_block.1 = (bf16[128,512]{1,0:T(8,128)(2,1)S(1)}, f32[128,512]{1,0:T(8,128)S(1)}, f32[128,1]{1,0:T(8,128)S(1)}, f32[128,512]{1,0:T(8,128)S(1)}) custom-call(s32[2]{0:T(128)S(1)} %pad_add_fusion.refs_0_, bf16[128,512]{1,0:T(8,128)(2,1)S(1)} %copy-done, bf16[512,128]{1,0:T(8,128)(2,1)S(1)} %slice_bitcast_fusion.1.refs_2_.refs_9_, ...), custom_call_target="tpu_custom_call" | custom-call | tf_op jit(solution)/shard_map/first_block/pallas_call | solution.py:259
  13.0 0.0 collective-permute-done.3.refs_14_
  13.1 0.0 collective-permute-done.5.refs_16_
  13.1 3.5 %rest.1 = (bf16[128,512]{1,0:T(8,128)(2,1)}, bf16[8,2,64,128]{3,2,1,0:T(8,128)(2,1)S(1)}) custom-call(s32[2]{0:T(128)S(1)} %pad_add_fusion.refs_0_, s32[16]{0:T(128)S(1)} %copy-done.2, bf16[128,512]{1,0:T(8,128)(2,1)S(1)} %copy-done, bf16[128,512]{1,0:T(8,128)(2,1)S(1)} %get-tuple-element.9.refs_3_, f32[128,512]{1,0:T(8,128)S(1)} %get-tuple-element.10.refs_4_, ...), custom_call_target="tpu_custom_call" | custom-call | tf_op jit(solution)/shard_map/rest/pallas_call | solution.py:270
  16.6 15.5 %all_to_all.5 = bf16[8,2,64,128]{3,2,1,0:T(8,128)(2,1)S(1)} all-to-all(bf16[8,2,64,128]{3,2,1,0:T(8,128)(2,1)S(1)} %get-tuple-element.14), channel_id=1, replica_groups=mesh['seq'=8,'mp'=4] {'seq'}, dimensions={0} | all-to-all | bytes 524288 | tf_op jit(solution)/shard_map/all_to_all | solution.py:299
  32.1 0.7 %pad.8 = f32[9,64,128]{2,1,0:T(8,128)} pad(f32[1,64,128]{2,1,0:T(8,128)S(1)} %get-tuple-element.15, f32[]{:T(128)} %constant.14.clone.1), padding=4_4x0_0x0_0 | pad | bytes 327684 | tf_op jit(solution)/shard_map/jit(_pad)/pad | solution.py:302
  32.8 0.7 %pad.7 = f32[9,64,128]{2,1,0:T(8,128)} pad(f32[1,64,128]{2,1,0:T(8,128)S(1)} %get-tuple-element.16, f32[]{:T(128)} %constant.14.clone.1), padding=4_4x0_0x0_0 | pad | bytes 327684 | tf_op jit(solution)/shard_map/jit(_pad)/pad | solution.py:302
  (6 shorter events, 0.1 us)
Async XLA Ops:
  0.6 12.4 %copy-start.1 = (bf16[512,5]{0,1:T(8,128)(2,1)S(1)}, bf16[512,5]{0,1:T(8,128)(2,1)}, u32[]{:S(2)}) copy-start(bf16[512,5]{0,1:T(8,128)(2,1)} %param.11) | copy-start | bytes 15364
  0.6 12.4 %copy-start.2 = (s32[16]{0:T(128)S(1)}, s32[16]{0:T(128)}, u32[]{:S(2)}) copy-start(s32[16]{0:T(128)} %refs_1_.3) | copy-start | bytes 196
  0.7 12.4 %copy-start.3 = (s32[128]{0:T(128)S(1)}, s32[128]{0:T(128)}, u32[]{:S(2)}) copy-start(s32[128]{0:T(128)} %param.7) | copy-start | bytes 1540
  1.6 6.9 %collective-permute-start.1 = (bf16[512,128]{1,0:T(8,128)(2,1)S(1)}, bf16[512,128]{1,0:T(8,128)(2,1)S(1)}, u32[]{:S(2)}, u32[]{:S(2)}) collective-permute-start(bf16[512,128]{1,0:T(8,128)(2,1)S(1)} %slice_bitcast_fusion.1.refs_2_.refs_9_), channel_id=1, source_target_pairs={{0,2},{1,3},{2,0},{3,1},{4,6},{5,7},{6,4},{7,5},{8,10},{9,11},{10,... | collective-permute-start | bytes 393224 | tf_op jit(solution)/shard_map/ppermute | solution.py:146
  5.5 5.4 %collective-permute-start.4 = (bf16[512,128]{1,0:T(8,128)(2,1)S(1)}, bf16[512,128]{1,0:T(8,128)(2,1)S(1)}, u32[]{:S(2)}, u32[]{:S(2)}) collective-permute-start(bf16[512,128]{1,0:T(8,128)(2,1)S(1)} %slice_bitcast_fusion.refs_13_), channel_id=1, source_target_pairs={{0,2},{1,3},{2,0},{3,1},{4,6},{5,7},{6,4},{7,5},{8,10},{9,11},{10,... | collective-permute-start | bytes 393224 | tf_op jit(solution)/shard_map/ppermute | solution.py:146
  5.6 5.4 %collective-permute-start = (bf16[512,128]{1,0:T(8,128)(2,1)S(1)}, bf16[512,128]{1,0:T(8,128)(2,1)S(1)}, u32[]{:S(2)}, u32[]{:S(2)}) collective-permute-start(bf16[512,128]{1,0:T(8,128)(2,1)S(1)} %slice_bitcast_fusion.1.refs_2_.refs_9_), channel_id=1, source_target_pairs={{0,1},{1,0},{2,3},{3,2},{4,5},{5,4},{6,7},{7,6},{8,9},{9,8},{10,11... | collective-permute-start | bytes 393224 | tf_op jit(solution)/shard_map/ppermute | solution.py:146
  8.5 2.5 %collective-permute-start.2 = (bf16[512,128]{1,0:T(8,128)(2,1)S(1)}, bf16[512,128]{1,0:T(8,128)(2,1)S(1)}, u32[]{:S(2)}, u32[]{:S(2)}) collective-permute-start(bf16[512,128]{1,0:T(8,128)(2,1)S(1)} %collective-permute-done.1.refs_4_.refs_11_), channel_id=1, source_target_pairs={{0,1},{1,0},{2,3},{3,2},{4,5},{5,4},{6,7},{7,6},{8,9},{9,8},{10,11... | collective-permute-start | bytes 393224 | tf_op jit(solution)/shard_map/ppermute | solution.py:146
  8.5 4.5 %collective-permute-start.3 = (bf16[512,128]{1,0:T(8,128)(2,1)S(1)}, bf16[512,128]{1,0:T(8,128)(2,1)S(1)}, u32[]{:S(2)}, u32[]{:S(2)}) collective-permute-start(bf16[512,128]{1,0:T(8,128)(2,1)S(1)} %slice_bitcast_fusion.refs_13_), channel_id=1, source_target_pairs={{0,1},{1,0},{2,3},{3,2},{4,5},{5,4},{6,7},{7,6},{8,9},{9,8},{10,11... | collective-permute-start | bytes 393224 | tf_op jit(solution)/shard_map/ppermute | solution.py:146
  10.9 2.1 %collective-permute-start.5 = (bf16[512,128]{1,0:T(8,128)(2,1)S(1)}, bf16[512,128]{1,0:T(8,128)(2,1)S(1)}, u32[]{:S(2)}, u32[]{:S(2)}) collective-permute-start(bf16[512,128]{1,0:T(8,128)(2,1)S(1)} %collective-permute-done.4.refs_15_), channel_id=1, source_target_pairs={{0,1},{1,0},{2,3},{3,2},{4,5},{5,4},{6,7},{7,6},{8,9},{9,8},{10,11... | collective-permute-start | bytes 393224 | tf_op jit(solution)/shard_map/ppermute | solution.py:146
  11.0 0.9 %copy-start = (bf16[128,512]{1,0:T(8,128)(2,1)S(1)}, bf16[128,512]{1,0:T(8,128)(2,1)}, u32[]{:S(2)}) copy-start(bf16[128,512]{1,0:T(8,128)(2,1)} %refs_2_.1) | copy-start | bytes 393220

commit v2 on v0

v2 whole, which is shorter than its diff:
```python
import functools

import jax
import jax.numpy as jnp
from jax import lax
from jax.experimental import pallas as pl
from jax.experimental.pallas import tpu as pltpu
from jax.sharding import PartitionSpec as P

DILATION_FIRST1 = 2048
DILATION_SECOND2 = 4096


epsilon = 1e-05
root_half = 0.7071067811865476
inv_root_two_pi = 0.3989422804014327
ROW_CHUNK = 32
SIDE_ROWS = 16
VMEM_LIMIT = 24 * 1024 * 1024


def gelu_parts(conv_out):
    normal_cdf = 0.5 * (1.0 + lax.erf(conv_out * root_half))
    gelu_slope = normal_cdf + conv_out * inv_root_two_pi * jnp.exp(-0.5 * conv_out * conv_out)
    return (conv_out * normal_cdf, gelu_slope)


def norm_parts(activation):
    values = activation.astype(jnp.float32)
    centre = jnp.mean(values, axis=-1, keepdims=True)
    centred = values - centre
    spread = jnp.mean(centred * centred, axis=-1, keepdims=True)
    inverse = lax.rsqrt(spread + epsilon)
    return (centred * inverse, inverse)


def active_hops(tap_count, dilation_blocks, seq_count):
    centre_tap = tap_count // 2
    hops = [(tap, dilation_blocks * (tap - centre_tap)) for tap in range(tap_count)]
    return [(tap, hop) for tap, hop in hops if abs(hop) < seq_count]


def shifted(x, axis, by):
    if by == 0:
        return x
    peers = lax.axis_size(axis)
    pairs = [(i, i + by) for i in range(peers) if 0 <= i + by < peers]
    return lax.ppermute(x, axis, pairs)


def loss_grad(hidden_top, targets, head_weight):
    logits = lax.dot_general(
        head_weight, hidden_top, (((0,), (1,)), ((), ())), preferred_element_type=jnp.float32
    )
    exponent = jnp.exp(logits)
    probability = exponent / jnp.sum(exponent, axis=0, keepdims=True)
    vocab_rows = lax.broadcasted_iota(jnp.int32, logits.shape, 0)
    onehot = (vocab_rows == targets[None, :]).astype(jnp.float32)
    weight = (targets >= 0).astype(jnp.float32)[None, :]
    dlogits = weight * (probability - onehot)
    return lax.dot_general(
        dlogits,
        head_weight.astype(jnp.float32),
        (((0,), (1,)), ((), ())),
        precision=lax.Precision.HIGHEST,
    )


def general_plan(hidden_entry_states, base_ids, mask_index, first_kernel, second_kernel, head_weight, first_hops, second_hops):
    seq_count = lax.axis_size("seq")
    rows_per_block, channels = hidden_entry_states.shape
    tap_count, _, own_width = first_kernel.shape
    mask_count = mask_index.shape[0]
    offsets = mask_index - lax.axis_index("seq") * rows_per_block
    positions = lax.broadcasted_iota(jnp.int32, (rows_per_block, mask_count), 0)
    masked = jnp.any(positions == offsets[None, :], axis=1)
    targets = jnp.where(masked, base_ids, -1)

    def used(kernel, hops):
        first_tap, last_tap = hops[0][0], hops[-1][0]
        return kernel[first_tap : last_tap + 1]

    def block_forward_pass(source, kernel, hops):
        stacked = jnp.concatenate([shifted(source, "seq", -hop) for _, hop in hops], axis=1)
        conv_out = jnp.dot(
            stacked,
            used(kernel, hops).reshape(len(hops) * channels, own_width),
            preferred_element_type=jnp.float32,
        )
        activation, gelu_slope = gelu_parts(conv_out)
        mixed_all = lax.all_gather(activation.astype(jnp.bfloat16), "mp", axis=1, tiled=True)
        normed, inverse = norm_parts(mixed_all)
        result = (source.astype(jnp.float32) + normed).astype(jnp.bfloat16)
        return (result, (source, normed, inverse, gelu_slope))

    def block_backward_pass(grad_out, saved, kernel, hops):
        source, normed, inverse, gelu_slope = saved
        mean_grad = jnp.mean(grad_out, axis=-1, keepdims=True)
        mean_cross = jnp.mean(grad_out * normed, axis=-1, keepdims=True)
        grad_act = inverse * (grad_out - mean_grad - normed * mean_cross)
        own_cols = lax.dynamic_slice_in_dim(
            grad_act, lax.axis_index("mp") * own_width, own_width, 1
        )
        grad_conv = (own_cols * gelu_slope).astype(jnp.bfloat16)
        tap_stack = jnp.stack([shifted(grad_conv, "seq", hop) for _, hop in hops], axis=0)
        input_part = jnp.einsum(
            "kro,kdo->rd", tap_stack, used(kernel, hops), preferred_element_type=jnp.float32
        )
        grad_in = grad_out + lax.psum(input_part.astype(jnp.bfloat16), "mp").astype(jnp.float32)
        kernel_part = jnp.einsum(
            "rd,kro->kdo", source, tap_stack, preferred_element_type=jnp.float32
        )
        by_owner = kernel_part.reshape(len(hops), seq_count, channels // seq_count, own_width)
        received = lax.all_to_all(
            by_owner.astype(jnp.bfloat16), "seq", split_axis=1, concat_axis=1, tiled=True
        ).astype(by_owner.dtype)
        first_tap, last_tap = hops[0][0], hops[-1][0]
        kernel_grad = jnp.pad(
            jnp.sum(received, axis=1),
            ((first_tap, tap_count - 1 - last_tap), (0, 0), (0, 0)),
        )
        return (grad_in, kernel_grad)

    hidden_one, saved_one = block_forward_pass(hidden_entry_states, first_kernel, first_hops)
    hidden_two, saved_two = block_forward_pass(hidden_one, second_kernel, second_hops)
    grad_two = loss_grad(hidden_two, targets, head_weight)
    grad_one, second_grad = block_backward_pass(grad_two, saved_two, second_kernel, second_hops)
    grad_zero, first_grad = block_backward_pass(grad_one, saved_one, first_kernel, first_hops)
    return (grad_zero.astype(jnp.bfloat16), first_grad, second_grad)


NN = (((1,), (0,)), ((), ()))
NT = (((1,), (1,)), ((), ()))
TN = (((0,), (0,)), ((), ()))


def dot(a, b, dims=NN):
    return lax.dot_general(a, b, dims, preferred_element_type=jnp.float32)


def xor_pairs(count, offset):
    return [(i, i ^ offset) for i in range(count)]


def block_at(me, offset, width):
    return pl.ds(pl.multiple_of((me ^ offset) * width, width), width)


def own_order(me, ref, rows, count):
    width = ref.shape[1] // count
    return jnp.concatenate([ref[rows, block_at(me, o, width)] for o in range(count)], axis=1)


def square(me, kernel_refs):
    width = kernel_refs[0].shape[1]
    count = len(kernel_refs)
    columns = [
        jnp.concatenate([ref[block_at(me, o, width), :] for o in range(count)], axis=0)
        for ref in kernel_refs
    ]
    return jnp.concatenate(columns, axis=1)


def row_chunks(rows, size):
    size = size if rows % size == 0 else rows
    return [pl.ds(start, size) for start in range(0, rows, size)]


def prepare_body(centre_tap, where_ref, mask_ref, ids_ref, source_ref, first_ref, second_ref, own_first_ref, own_second_ref, both_ref, rows_ref, sems):
    rows = source_ref.shape[0]
    copies = [
        pltpu.make_async_copy(first_ref.at[centre_tap], own_first_ref, sems.at[0]),
        pltpu.make_async_copy(second_ref.at[centre_tap], own_second_ref, sems.at[1]),
        pltpu.make_async_copy(source_ref, rows_ref.at[pl.ds(0, rows)], sems.at[2]),
    ]
    for copy in copies:
        copy.start()
    positions = lax.broadcasted_iota(jnp.int32, ids_ref.shape, 1) + where_ref[1] * rows
    masked = jnp.zeros(ids_ref.shape, jnp.int32)
    for entry in range(mask_ref.shape[0]):
        masked = jnp.where(positions == mask_ref[entry], 1, masked)
    targets = jnp.where(masked == 1, ids_ref[...], -1).astype(jnp.float32)
    extra = rows_ref.shape[0] - rows
    rows_ref[rows:, :] = jnp.zeros((extra, rows_ref.shape[1]), jnp.bfloat16)
    rows_ref[rows:, 0:rows] = jnp.broadcast_to(targets, (extra, rows)).astype(jnp.bfloat16)
    for copy in copies:
        copy.wait()
    both_ref[0] = own_first_ref[...]
    both_ref[1] = own_second_ref[...]


def first_block_body(count, where_ref, own_ref, peer_ref, head_ref, *refs):
    kernel_refs = refs[:count]
    hidden_ref, normed_ref, scale_ref, hidden_flip_ref, source_flip_ref, head_out_ref = refs[count:]
    me = where_ref[0]
    half = hidden_ref.shape[0] // 2
    width = kernel_refs[0].shape[1]
    weights = square(me, kernel_refs)
    for part, ref in enumerate((own_ref, peer_ref)):
        conv_out = dot(own_order(me, ref, pl.ds(0, half), count), weights)
        for start in range(0, half, ROW_CHUNK):
            rows = pl.ds(part * half + start, ROW_CHUNK)
            activation, gelu_slope = gelu_parts(conv_out[start : start + ROW_CHUNK])
            normed, inverse = norm_parts(activation.astype(jnp.bfloat16))
            scale_ref[rows, :] = gelu_slope * inverse
            normed_ref[rows, :] = normed
            source = own_order(me, ref, pl.ds(start, ROW_CHUNK), count)
            hidden_ref[rows, :] = (source.astype(jnp.float32) + normed).astype(jnp.bfloat16)
        source_flip_ref[:, pl.ds(part * half, half)] = ref[pl.ds(0, half), :].T
    for offset in range(count):
        flipped = hidden_ref[:, pl.ds(offset * width, width)].T
        hidden_flip_ref[block_at(me, offset, width), :] = flipped
    head_out_ref[...] = jnp.zeros_like(head_out_ref)
    classes = head_ref.shape[0]
    head_out_ref[0:classes, :] = own_order(me, head_ref, pl.ds(0, classes), count)


def rest_body(count, classes, where_ref, own_ref, peer_ref, head_ref, hidden_one_ref, normed_one_ref, scale_one_ref, hidden_flip_ref, source_flip_ref, *refs):
    kernel_refs = refs[:count]
    self_ref = refs[count]
    sent_refs = refs[count + 1 : -7]
    grad_out_ref, grad_conv_out_ref = refs[-7:-5]
    normed_two_ref, scale_two_ref, hidden_two_ref, grad_ref, grad_conv_ref = refs[-5:]
    me, block = where_ref[0], where_ref[1]
    total_rows = hidden_one_ref.shape[0]
    half = total_rows // 2
    width = kernel_refs[0].shape[1]
    depth = self_ref.shape[1]
    weights = square(me, kernel_refs)
    for start in range(0, total_rows, half):
        conv_out = dot(hidden_one_ref[pl.ds(start, half), :], weights)
        for inner in range(0, half, ROW_CHUNK):
            rows = pl.ds(start + inner, ROW_CHUNK)
            activation, gelu_slope = gelu_parts(conv_out[inner : inner + ROW_CHUNK])
            normed, inverse = norm_parts(activation.astype(jnp.bfloat16))
            scale_two_ref[rows, :] = gelu_slope * inverse
            normed_two_ref[rows, :] = normed
            hidden_two_ref[rows, :] = (hidden_one_ref[rows, :].astype(jnp.float32) + normed).astype(jnp.bfloat16)

    head = head_ref[...]
    logits = dot(head, hidden_two_ref[...], NT)
    class_rows = lax.broadcasted_iota(jnp.int32, logits.shape, 0)
    exponent = jnp.where(class_rows < classes, jnp.exp(logits), 0.0)
    probability = exponent / jnp.sum(exponent, axis=0, keepdims=True)
    targets = jnp.concatenate(
        [ref[half : half + head.shape[0], 0:half] for ref in (own_ref, peer_ref)], axis=1
    ).astype(jnp.float32)
    onehot = (class_rows.astype(jnp.float32) == targets).astype(jnp.float32)
    weight = (targets >= 0.0).astype(jnp.float32)
    rest = jnp.where(class_rows < classes, weight * (probability - onehot), 0.0)
    terms = []
    for _ in range(3):
        term = rest.astype(jnp.bfloat16)
        terms.append(term)
        rest = rest - term.astype(jnp.float32)
    grad_ref[...] = dot(jnp.concatenate(terms, axis=0), jnp.concatenate([head] * 3, axis=0), TN)

    def norm_backward(normed_ref, scale_ref):
        for rows in row_chunks(total_rows, ROW_CHUNK):
            grad_out, normed = grad_ref[rows, :], normed_ref[rows, :]
            mean_grad = jnp.mean(grad_out, axis=-1, keepdims=True)
            mean_cross = jnp.mean(grad_out * normed, axis=-1, keepdims=True)
            grad_conv_ref[rows, :] = (
                (grad_out - mean_grad - normed * mean_cross) * scale_ref[rows, :]
            ).astype(jnp.bfloat16)

    def kernel_parts(flip_ref, slot):
        owners = 1 + len(sent_refs)
        sources = [
            flip_ref[pl.ds(pl.multiple_of((block ^ (2 * j)) * depth, depth), depth), :]
            for j in range(owners)
        ]
        part = dot(jnp.concatenate(sources, axis=0), grad_conv_ref[:, 0:width])
        self_ref[slot] = part[0:depth]
        for j, ref in enumerate(sent_refs):
            ref[slot] = part[(j + 1) * depth : (j + 2) * depth].astype(jnp.bfloat16)

    norm_backward(normed_two_ref, scale_two_ref)
    for start in range(0, total_rows, half):
        rows = pl.ds(start, half)
        grad_ref[rows, :] += dot(grad_conv_ref[rows, :], weights, NT)
    kernel_parts(hidden_flip_ref, 1)
    norm_backward(normed_one_ref, scale_one_ref)
    kernel_parts(source_flip_ref, 0)
    grad_out_ref[...] = grad_ref[pl.ds(0, half), :]
    grad_conv_out_ref[...] = grad_conv_ref[pl.ds(0, half), :]


def input_grad_body(count, where_ref, grad_ref, grad_conv_ref, *refs):
    kernel_refs = refs[:count]
    input_grad_ref, first_ref, second_ref = refs[count:]
    me = where_ref[0]
    width = kernel_refs[0].shape[1]
    total = grad_ref[...] + dot(grad_conv_ref[...], square(me, kernel_refs), NT)
    for offset in range(count):
        input_grad_ref[:, block_at(me, offset, width)] = total[
            :, offset * width : (offset + 1) * width
        ].astype(jnp.bfloat16)
    first_ref[...] = jnp.zeros_like(first_ref)
    second_ref[...] = jnp.zeros_like(second_ref)


def total_body(centre_tap, first_in_ref, second_in_ref, self_ref, *refs):
    received = refs[:-4]
    first_ref, second_ref, sum_ref, sems = refs[-4:]
    sum_ref[...] = self_ref[...] + sum(ref[...].astype(jnp.float32) for ref in received)
    copies = [
        pltpu.make_async_copy(sum_ref.at[slot], ref.at[centre_tap], sems.at[slot])
        for slot, ref in enumerate((first_ref, second_ref))
    ]
    for copy in copies:
        copy.start()
    for copy in copies:
        copy.wait()


def local_plan(hidden_entry_states, base_ids, mask_index, first_kernel, second_kernel, head_weight):
    seq_count = lax.axis_size("seq")
    mp_count = lax.axis_size("mp")
    rows, channels = hidden_entry_states.shape
    tap_count, _, width = first_kernel.shape
    classes = head_weight.shape[1]
    centre_tap = tap_count // 2
    depth = channels // seq_count
    where = jnp.stack([lax.axis_index("mp"), lax.axis_index("seq")]).astype(jnp.int32)

    vmem = pl.BlockSpec(memory_space=pltpu.VMEM)
    smem = pl.BlockSpec(memory_space=pltpu.SMEM)
    anywhere = pl.BlockSpec(memory_space=pl.ANY)

    def shape(dims, dtype=jnp.bfloat16):
        return jax.ShapeDtypeStruct(dims, dtype)

    def call(body, name, in_specs, out_shape, out_specs=None, scratch=(), aliases={}, flops=0, moved=0):
        return pl.pallas_call(
            body,
            out_shape=out_shape,
            in_specs=in_specs,
            out_specs=(vmem,) * len(out_shape) if out_specs is None else out_specs,
            scratch_shapes=list(scratch),
            input_output_aliases=aliases,
            compiler_params=pltpu.CompilerParams(vmem_limit_bytes=VMEM_LIMIT),
            cost_estimate=pl.CostEstimate(flops=flops, bytes_accessed=moved, transcendentals=0),
            name=name,
        )

    own_first, own_second, own_both, own_rows = call(
        functools.partial(prepare_body, centre_tap),
        "prepare",
        [smem, smem, vmem, anywhere, anywhere, anywhere],
        (shape((channels, width)), shape((channels, width)), shape((2, channels, width)), shape((rows + SIDE_ROWS, channels))),
        scratch=[pltpu.SemaphoreType.DMA((3,))],
    )(where, mask_index, base_ids[None, :], hidden_entry_states, first_kernel, second_kernel)

    first, second = {0: own_first}, {0: own_second}
    bit = far = mp_count // 2
    while bit:
        pairs = xor_pairs(mp_count, bit)
        for offset in list(first):
            if offset == 0 and bit != far:
                both = lax.ppermute(own_both, "mp", pairs)
                first[bit], second[bit] = both[0], both[1]
            else:
                first[offset ^ bit] = lax.ppermute(first[offset], "mp", pairs)
                second[offset ^ bit] = lax.ppermute(second[offset], "mp", pairs)
        bit //= 2
    first = [first[offset] for offset in range(mp_count)]
    second = [second[offset] for offset in range(mp_count)]
    peer_rows = lax.ppermute(own_rows, "seq", xor_pairs(seq_count, 1))

    pair_rows = 2 * rows
    wide = shape((pair_rows, channels), jnp.float32)
    half = shape((pair_rows, channels))
    flip = shape((channels, pair_rows))
    product = 2 * pair_rows * channels * channels
    hidden_one, normed_one, scale_one, hidden_flip, source_flip, head = call(
        functools.partial(first_block_body, mp_count),
        "first_block",
        [smem] + [vmem] * (3 + mp_count),
        (half, wide, wide, flip, flip, shape((SIDE_ROWS, channels))),
        flops=product,
        moved=4 * pair_rows * channels,
    )(where, own_rows, peer_rows, head_weight.T, *first)

    sent_count = seq_count // 2 - 1
    part = (2, depth, width)
    outs = call(
        functools.partial(rest_body, mp_count, classes),
        "rest",
        [smem] + [vmem] * (8 + mp_count),
        (shape(part, jnp.float32),) + (shape(part),) * sent_count + (shape((rows, channels), jnp.float32), shape((rows, channels))),
        scratch=[
            pltpu.VMEM((pair_rows, channels), jnp.float32),
            pltpu.VMEM((pair_rows, channels), jnp.float32),
            pltpu.VMEM((pair_rows, channels), jnp.bfloat16),
            pltpu.VMEM((pair_rows, channels), jnp.float32),
            pltpu.VMEM((pair_rows, channels), jnp.bfloat16),
        ],
        flops=3 * product,
        moved=16 * pair_rows * channels,
    )(where, own_rows, peer_rows, head, hidden_one, normed_one, scale_one, hidden_flip, source_flip, *second)
    own_part, sent, (grad_one, grad_conv) = outs[0], outs[1:-2], outs[-2:]

    received = [
        lax.ppermute(piece, "seq", xor_pairs(seq_count, 2 * (j + 1))) for j, piece in enumerate(sent)
    ]
    whole = shape((tap_count, depth, width), jnp.float32)
    input_grad, first_grad, second_grad = call(
        functools.partial(input_grad_body, mp_count),
        "input_grad",
        [smem] + [vmem] * (2 + mp_count),
        (shape((rows, channels)), whole, whole),
        flops=product // 2,
        moved=8 * rows * channels,
    )(where, grad_one, grad_conv, *first)
    first_grad, second_grad = call(
        functools.partial(total_body, centre_tap),
        "total",
        [anywhere, anywhere] + [vmem] * (1 + sent_count),
        (whole, whole),
        out_specs=(anywhere, anywhere),
        scratch=[pltpu.VMEM(part, jnp.float32), pltpu.SemaphoreType.DMA((2,))],
        aliases={0: 0, 1: 1},
    )(first_grad, second_grad, own_part, *received)
    return (input_grad, first_grad, second_grad)


def power_of_two(count):
    return count & (count - 1) == 0


def local(hidden_entry_states, base_ids, mask_index, first_kernel, second_kernel, head_weight):
    rows, channels = hidden_entry_states.shape
    tap_count, _, width = first_kernel.shape
    seq_count = lax.axis_size("seq")
    mp_count = lax.axis_size("mp")
    first_hops = active_hops(tap_count, DILATION_FIRST1 // rows, seq_count)
    second_hops = active_hops(tap_count, DILATION_SECOND2 // rows, seq_count)
    args = (hidden_entry_states, base_ids, mask_index, first_kernel, second_kernel, head_weight)
    fits = (
        power_of_two(mp_count)
        and power_of_two(seq_count)
        and seq_count > 1
        and width % 128 == 0
        and rows % 128 == 0
        and rows <= channels
        and (channels // seq_count) % 16 == 0
        and head_weight.shape[1] <= SIDE_ROWS
    )
    if len(first_hops) == 1 and len(second_hops) == 1 and fits:
        return local_plan(*args)
    return general_plan(*args, first_hops, second_hops)


def solution(mesh):
    placed = (P("seq", None), P("seq"), P("seq"), P(None, None, "mp"), P(None, None, "mp"), P())
    return jax.shard_map(
        local,
        mesh=mesh,
        in_specs=placed,
        out_specs=(P("seq", None), P(None, "seq", "mp"), P(None, "seq", "mp")),
        check_vma=False,
    )
```

time: 133 us -> 32.9 us (0.25)
  waiting for transfers between devices: 68.4 us -> 10.3 us
  between operations: 14.3 us -> 0.69 us
  blocking collectives: 12.1 us -> 0 us
  matrix products: 9.42 us -> 0 us
  other arithmetic: 7.94 us -> 0.08 us
  Pallas kernels: 0 us -> 7.17 us
  local copies, waits for them, and re-layouts: 8.16 us -> 4.78 us
  starting transfers between devices: 11.8 us -> 9.66 us
    psum x2 -> x0, waiting for transfers between devices: 68.4 us -> none  [block_backward_pass(): lax.psum(input_part.astype(jnp.bfloat16), 'mp').astype(jnp.float32)]
    all_gather x2 -> x0, blocking collectives: 12.1 us -> none  [block_forward_pass(): lax.all_gather(activation.astype(jnp.bfloat16), 'mp', axis=1, tiled=True)]
    all_to_all x2 -> x0, starting transfers between devices: 11.7 us -> none  [block_backward_pass(): lax.all_to_all(by_owner.astype(jnp.bfloat16), 'seq', split_axis=1, concat...]
    ppermute x0 -> x9, waiting for transfers between devices: none -> 10.3 us  [the longest x3 4.18 us: local_plan(): lax.ppermute(piece, 'seq', xor_pairs(seq_count, 2 * (j + 1)))]
    ppermute x0 -> x9, starting transfers between devices: none -> 9.66 us  [the longest x3 4.49 us: local_plan(): lax.ppermute(piece, 'seq', xor_pairs(seq_count, 2 * (j + 1)))]
    dot_general x8 -> x0, matrix products: 9.42 us -> none  [the longest x2 3.77 us: block_backward_pass(): jnp.einsum('kro,kdo->rd', tap_stack, kernel, preferred_element_type=jnp.f...]
    pallas_call x0 -> x5, Pallas kernels: none -> 7.17 us  [the longest x1 2.51 us: local_plan(): call(functools.partial(rest_body, mp_count, classes), 'rest', [smem] + [v...]
    convert_element_type x4 -> x0, local copies, waits for them, and re-layouts: 4.65 us -> none  [block_backward_pass(): by_owner.astype(jnp.bfloat16)]
  transfers between devices with their start and end apart: 4 -> 9, of which waited for: 2 -> 5; matrix products, arithmetic and copies ran while one was open for 10% -> 0% of each run, Pallas kernels for 0% -> 9%
where the time goes in v2:
time: 32.9 us; the launch traced here: 32.7 us
  waiting for transfers between devices  10.3 us (31%)
  starting transfers between devices  9.66 us (29%)
  Pallas kernels  7.17 us (22%)
  local copies, waits for them, and re-layouts  4.78 us (15%)
  between operations  0.69 us (2%)
    unnamed x12, local copies, waits for them, and re-layouts  4.76 us
    ppermute x3, starting transfers between devices, local_plan(): lax.ppermute(piece, 'seq', xor_pairs(seq_count, 2 * (j + 1)))  4.49 us
    ppermute x3, waiting for transfers between devices, local_plan(): lax.ppermute(piece, 'seq', xor_pairs(seq_count, 2 * (j + 1)))  4.18 us
    ppermute x2, waiting for transfers between devices, local_plan(): first[offset ^ bit] = lax.ppermute(first[offset], 'mp', pairs)  3.86 us
    ppermute x2, starting transfers between devices, local_plan(): second[offset ^ bit] = lax.ppermute(second[offset], 'mp', pairs)  2.56 us
    pallas_call x1, Pallas kernels, local_plan(): call(functools.partial(rest_body, mp_count, classes), 'rest', [smem] + [v...  2.51 us
    ppermute x2, waiting for transfers between devices, local_plan(): second[offset ^ bit] = lax.ppermute(second[offset], 'mp', pairs)  2.3 us
    ppermute x1, starting transfers between devices, local_plan(): peer_rows = lax.ppermute(own_rows, 'seq', xor_pairs(seq_count, 1))  1.98 us
  transfers between devices with their start and end apart: 9, of which 5 were waited for; matrix products, arithmetic and copies ran while one was open for 0% of the time, Pallas kernels for 9%

profile of v2, /device:TPU:0, one launch (start us, length us, event | category | flops | bytes accessed | tf_op | source)
XLA Modules:
  0.0 32.7 jit_solution(7000623509055658648)
XLA Ops:
  0.6 0.1 pad_add_fusion.where_ref
  0.7 1.3 %copy-done = bf16[9,512,128]{2,1,0:T(8,128)(2,1)S(1)} copy-done((bf16[9,512,128]{2,1,0:T(8,128)(2,1)S(1)}, bf16[9,512,128]{2,1,0:T(8,128)(2,1)}, u32[]{:S(2)}) %copy-start) | copy-done | bytes 1179672
  2.0 1.3 %copy-done.1 = bf16[9,512,128]{2,1,0:T(8,128)(2,1)S(1)} copy-done((bf16[9,512,128]{2,1,0:T(8,128)(2,1)S(1)}, bf16[9,512,128]{2,1,0:T(8,128)(2,1)}, u32[]{:S(2)}) %copy-start.1) | copy-done | bytes 1179672
  3.3 0.9 %copy-done.2 = bf16[128,512]{1,0:T(8,128)(2,1)S(1)} copy-done((bf16[128,512]{1,0:T(8,128)(2,1)S(1)}, bf16[128,512]{1,0:T(8,128)(2,1)}, u32[]{:S(2)}) %copy-start.2) | copy-done | bytes 131096
  4.2 0.7 %copy-done.4 = s32[16]{0:T(128)S(1)} copy-done((s32[16]{0:T(128)S(1)}, s32[16]{0:T(128)}, u32[]{:S(2)}) %copy-start.4) | copy-done | bytes 88
  4.8 0.7 %copy-done.5 = s32[128]{0:T(128)S(1)} copy-done((s32[128]{0:T(128)S(1)}, s32[128]{0:T(128)}, u32[]{:S(2)}) %copy-start.5) | copy-done | bytes 536
  5.5 1.1 %prepare.1 = (bf16[512,128]{1,0:T(8,128)(2,1)S(1)}, bf16[512,128]{1,0:T(8,128)(2,1)S(1)}, bf16[2,512,128]{2,1,0:T(8,128)(2,1)S(1)}, bf16[144,512]{1,0:T(8,128)(2,1)S(1)}) custom-call(s32[2]{0:T(128)S(1)} %pad_add_fusion.where_ref, s32[16]{0:T(128)S(1)} %copy-done.4, s32[1,128]{1,0:T(1,128)S(1)} %bitcast.9, bf16[128,512]{1,0:T(8,128)(2,1)S(1)} %copy-done.2, ...), custom_call_target="tpu_custom_call" | custom-call | tf_op jit(solution)/shard_map/prepare/pallas_call | solution.py:347
  6.6 0.6 %collective-permute-start.1 = (bf16[2,512,128]{2,1,0:T(8,128)(2,1)S(1)}, bf16[2,512,128]{2,1,0:T(8,128)(2,1)S(1)}, u32[]{:S(2)}, u32[]{:S(2)}) collective-permute-start(bf16[2,512,128]{2,1,0:T(8,128)(2,1)S(1)} %get-tuple-element.26), channel_id=1, source_target_pairs={{0,1},{1,0},{2,3},{3,2},{4,5},{5,4},{6,7},{7,6},{8,9},{9,8},{10,11... | collective-permute-start | bytes 786440 | tf_op jit(solution)/shard_map/ppermute | solution.py:361
  7.2 2.6 %collective-permute-start.4 = (bf16[512,128]{1,0:T(8,128)(2,1)S(1)}, bf16[512,128]{1,0:T(8,128)(2,1)S(1)}, u32[]{:S(2)}, u32[]{:S(2)}) collective-permute-start(bf16[512,128]{1,0:T(8,128)(2,1)S(1)} %get-tuple-element.33.refs_0_), channel_id=1, source_target_pairs={{0,2},{1,3},{2,0},{3,1},{4,6},{5,7},{6,4},{7,5},{8,10},{9,11},{10,... | collective-permute-start | bytes 393224 | tf_op jit(solution)/shard_map/ppermute | solution.py:365
  9.7 0.1 collective-permute-start.2
  9.8 2.0 %collective-permute-start = (bf16[144,512]{1,0:T(8,128)(2,1)S(1)}, bf16[144,512]{1,0:T(8,128)(2,1)S(1)}, u32[]{:S(2)}, u32[]{:S(2)}) collective-permute-start(bf16[144,512]{1,0:T(8,128)(2,1)S(1)} %get-tuple-element.24.own_ref), channel_id=1, source_target_pairs={{0,4},{4,0},{8,12},{12,8},{16,20},{20,16},{24,28},{28,24},{1,5},{5... | collective-permute-start | bytes 442376 | tf_op jit(solution)/shard_map/ppermute | solution.py:369
  11.8 2.3 %collective-permute-done.4.refs_2_ = bf16[512,128]{1,0:T(8,128)(2,1)S(1)} collective-permute-done((bf16[512,128]{1,0:T(8,128)(2,1)S(1)}, bf16[512,128]{1,0:T(8,128)(2,1)S(1)}, u32[]{:S(2)}, u32[]{:S(2)}) %collective-permute-start.4) | collective-permute-done | bytes 131104 | tf_op jit(solution)/shard_map/ppermute | solution.py:365
  14.1 2.5 %collective-permute-done.2.refs_2_ = bf16[512,128]{1,0:T(8,128)(2,1)S(1)} collective-permute-done((bf16[512,128]{1,0:T(8,128)(2,1)S(1)}, bf16[512,128]{1,0:T(8,128)(2,1)S(1)}, u32[]{:S(2)}, u32[]{:S(2)}) %collective-permute-start.2) | collective-permute-done | bytes 131104 | tf_op jit(solution)/shard_map/ppermute | solution.py:364
  16.6 0.0 collective-permute-start.3
  16.6 0.0 collective-permute-done.1
  16.6 1.3 %collective-permute-done.3.refs_3_ = bf16[512,128]{1,0:T(8,128)(2,1)S(1)} collective-permute-done((bf16[512,128]{1,0:T(8,128)(2,1)S(1)}, bf16[512,128]{1,0:T(8,128)(2,1)S(1)}, u32[]{:S(2)}, u32[]{:S(2)}) %collective-permute-start.3) | collective-permute-done | bytes 131104 | tf_op jit(solution)/shard_map/ppermute | solution.py:364
  18.0 1.3 %first_block.1 = (bf16[256,512]{1,0:T(8,128)(2,1)S(1)}, f32[256,512]{1,0:T(8,128)S(1)}, f32[256,512]{1,0:T(8,128)S(1)}, bf16[512,256]{1,0:T(8,128)(2,1)S(1)}, bf...) custom-call(s32[2]{0:T(128)S(1)} %pad_add_fusion.where_ref, bf16[144,512]{1,0:T(8,128)(2,1)S(1)} %get-tuple-element.24.own_ref, ...), custom_call_target="tpu_custom_call" | custom-call | flops 134217728 | bytes 524288 | tf_op jit(solution)/shard_map/first_block/pallas_call | solution.py:376
  19.3 2.5 %rest.1 = (f32[2,64,128]{2,1,0:T(8,128)S(1)}, bf16[2,64,128]{2,1,0:T(8,128)(2,1)S(1)}, bf16[2,64,128]{2,1,0:T(8,128)(2,1)S(1)}, bf16[2,64,128]{2,1,0:T(8,128)(2,...) custom-call(s32[2]{0:T(128)S(1)} %pad_add_fusion.where_ref, ...), custom_call_target="tpu_custom_call" | custom-call | flops 402653184 | bytes 2097152 | tf_op jit(solution)/shard_map/rest/pallas_call | solution.py:387
  21.8 1.9 %collective-permute-start.6 = (bf16[2,64,128]{2,1,0:T(8,128)(2,1)S(1)}, bf16[2,64,128]{2,1,0:T(8,128)(2,1)S(1)}, u32[]{:S(2)}, u32[]{:S(2)}) collective-permute-start(bf16[2,64,128]{2,1,0:T(8,128)(2,1)S(1)} %get-tuple-element.40), channel_id=1, source_target_pairs={{0,8},{4,12},{8,0},{12,4},{16,24},{20,28},{24,16},{28,20},{1,9},{5... | collective-permute-start | bytes 98312 | tf_op jit(solution)/shard_map/ppermute | solution.py:405
  23.7 2.6 %collective-permute-start.7 = (bf16[2,64,128]{2,1,0:T(8,128)(2,1)S(1)}, bf16[2,64,128]{2,1,0:T(8,128)(2,1)S(1)}, u32[]{:S(2)}, u32[]{:S(2)}) collective-permute-start(bf16[2,64,128]{2,1,0:T(8,128)(2,1)S(1)} %get-tuple-element.41), channel_id=1, source_target_pairs={{0,16},{4,20},{8,24},{12,28},{16,0},{20,4},{24,8},{28,12},{1,17},{... | collective-permute-start | bytes 98312 | tf_op jit(solution)/shard_map/ppermute | solution.py:405
  26.3 1.5 %input_grad.1 = (bf16[128,512]{1,0:T(8,128)(2,1)}, f32[9,64,128]{2,1,0:T(8,128)}, f32[9,64,128]{2,1,0:T(8,128)}) custom-call(s32[2]{0:T(128)S(1)} %pad_add_fusion.where_ref, f32[128,512]{1,0:T(8,128)S(1)} %get-tuple-element.34.grad_ref, bf16[128,512]{1,0:T(8,128)(2,1)S(1)} %get-tuple-element.35.grad_conv_ref, ...), custom_call_target="tpu_custom_call" | custom-call | flops 67108864 | bytes 524288 | tf_op jit(solution)/shard_map/input_grad/pallas_call | solution.py:408
  27.9 1.3 %collective-permute-done.7.refs_1_ = bf16[2,64,128]{2,1,0:T(8,128)(2,1)S(1)} collective-permute-done((bf16[2,64,128]{2,1,0:T(8,128)(2,1)S(1)}, bf16[2,64,128]{2,1,0:T(8,128)(2,1)S(1)}, u32[]{:S(2)}, u32[]{:S(2)}) %collective-permute-start.7) | collective-permute-done | bytes 32800 | tf_op jit(solution)/shard_map/ppermute | solution.py:405
  29.1 2.9 %collective-permute-done.8.refs_2_ = bf16[2,64,128]{2,1,0:T(8,128)(2,1)S(1)} collective-permute-done((bf16[2,64,128]{2,1,0:T(8,128)(2,1)S(1)}, bf16[2,64,128]{2,1,0:T(8,128)(2,1)S(1)}, u32[]{:S(2)}, u32[]{:S(2)}) %collective-permute-start.8) | collective-permute-done | bytes 32800 | tf_op jit(solution)/shard_map/ppermute | solution.py:405
  32.0 0.7 %total.1 = (f32[9,64,128]{2,1,0:T(8,128)}, f32[9,64,128]{2,1,0:T(8,128)}) custom-call(f32[9,64,128]{2,1,0:T(8,128)} %get-tuple-element.37.first_in_ref, f32[9,64,128]{2,1,0:T(8,128)} %get-tuple-element.38.second_in_ref, f32[2,64,128]{2,1,0:T(8,128)S(1)} %get-tuple-element.39.self_ref, ...), custom_call_target="tpu_custom_call", output_to_operand_aliasing={{0}: (0, {}), {1}: (1, {})} | custom-call | tf_op jit(solution)/shard_map/total/pallas_call | solution.py:416
  (13 shorter events, 0.0 us)
Async XLA Ops:
  0.7 1.3 %copy-start = (bf16[9,512,128]{2,1,0:T(8,128)(2,1)S(1)}, bf16[9,512,128]{2,1,0:T(8,128)(2,1)}, u32[]{:S(2)}) copy-start(bf16[9,512,128]{2,1,0:T(8,128)(2,1)} %first_ref.1) | copy-start | bytes 3538948
  2.0 1.3 %copy-start.1 = (bf16[9,512,128]{2,1,0:T(8,128)(2,1)S(1)}, bf16[9,512,128]{2,1,0:T(8,128)(2,1)}, u32[]{:S(2)}) copy-start(bf16[9,512,128]{2,1,0:T(8,128)(2,1)} %second_ref.1) | copy-start | bytes 3538948
  3.3 0.9 %copy-start.2 = (bf16[128,512]{1,0:T(8,128)(2,1)S(1)}, bf16[128,512]{1,0:T(8,128)(2,1)}, u32[]{:S(2)}) copy-start(bf16[128,512]{1,0:T(8,128)(2,1)} %source_ref.1) | copy-start | bytes 393220
  4.2 0.7 %copy-start.4 = (s32[16]{0:T(128)S(1)}, s32[16]{0:T(128)}, u32[]{:S(2)}) copy-start(s32[16]{0:T(128)} %mask_ref.1) | copy-start | bytes 196
  4.8 0.7 %copy-start.5 = (s32[128]{0:T(128)S(1)}, s32[128]{0:T(128)}, u32[]{:S(2)}) copy-start(s32[128]{0:T(128)} %param.7) | copy-start | bytes 1540
  5.5 12.5 %copy-start.3 = (bf16[512,5]{0,1:T(8,128)(2,1)S(1)}, bf16[512,5]{0,1:T(8,128)(2,1)}, u32[]{:S(2)}) copy-start(bf16[512,5]{0,1:T(8,128)(2,1)} %param.11) | copy-start | bytes 15364
  6.6 10.0 %collective-permute-start.1 = (bf16[2,512,128]{2,1,0:T(8,128)(2,1)S(1)}, bf16[2,512,128]{2,1,0:T(8,128)(2,1)S(1)}, u32[]{:S(2)}, u32[]{:S(2)}) collective-permute-start(bf16[2,512,128]{2,1,0:T(8,128)(2,1)S(1)} %get-tuple-element.26), channel_id=1, source_target_pairs={{0,1},{1,0},{2,3},{3,2},{4,5},{5,4},{6,7},{7,6},{8,9},{9,8},{10,11... | collective-permute-start | bytes 786440 | tf_op jit(solution)/shard_map/ppermute | solution.py:361
  7.2 6.9 %collective-permute-start.4 = (bf16[512,128]{1,0:T(8,128)(2,1)S(1)}, bf16[512,128]{1,0:T(8,128)(2,1)S(1)}, u32[]{:S(2)}, u32[]{:S(2)}) collective-permute-start(bf16[512,128]{1,0:T(8,128)(2,1)S(1)} %get-tuple-element.33.refs_0_), channel_id=1, source_target_pairs={{0,2},{1,3},{2,0},{3,1},{4,6},{5,7},{6,4},{7,5},{8,10},{9,11},{10,... | collective-permute-start | bytes 393224 | tf_op jit(solution)/shard_map/ppermute | solution.py:365
  9.7 6.9 %collective-permute-start.2 = (bf16[512,128]{1,0:T(8,128)(2,1)S(1)}, bf16[512,128]{1,0:T(8,128)(2,1)S(1)}, u32[]{:S(2)}, u32[]{:S(2)}) collective-permute-start(bf16[512,128]{1,0:T(8,128)(2,1)S(1)} %get-tuple-element.25.refs_0_), channel_id=1, source_target_pairs={{0,2},{1,3},{2,0},{3,1},{4,6},{5,7},{6,4},{7,5},{8,10},{9,11},{10,... | collective-permute-start | bytes 393224 | tf_op jit(solution)/shard_map/ppermute | solution.py:364
  9.8 6.9 %collective-permute-start = (bf16[144,512]{1,0:T(8,128)(2,1)S(1)}, bf16[144,512]{1,0:T(8,128)(2,1)S(1)}, u32[]{:S(2)}, u32[]{:S(2)}) collective-permute-start(bf16[144,512]{1,0:T(8,128)(2,1)S(1)} %get-tuple-element.24.own_ref), channel_id=1, source_target_pairs={{0,4},{4,0},{8,12},{12,8},{16,20},{20,16},{24,28},{28,24},{1,5},{5... | collective-permute-start | bytes 442376 | tf_op jit(solution)/shard_map/ppermute | solution.py:369
  14.1 5.3 %collective-permute-start.5 = (bf16[512,128]{1,0:T(8,128)(2,1)S(1)}, bf16[512,128]{1,0:T(8,128)(2,1)S(1)}, u32[]{:S(2)}, u32[]{:S(2)}) collective-permute-start(bf16[512,128]{1,0:T(8,128)(2,1)S(1)} %collective-permute-done.4.refs_2_), channel_id=1, source_target_pairs={{0,1},{1,0},{2,3},{3,2},{4,5},{5,4},{6,7},{7,6},{8,9},{9,8},{10,11... | collective-permute-start | bytes 393224 | tf_op jit(solution)/shard_map/ppermute | solution.py:365
  16.6 1.3 %collective-permute-start.3 = (bf16[512,128]{1,0:T(8,128)(2,1)S(1)}, bf16[512,128]{1,0:T(8,128)(2,1)S(1)}, u32[]{:S(2)}, u32[]{:S(2)}) collective-permute-start(bf16[512,128]{1,0:T(8,128)(2,1)S(1)} %collective-permute-done.2.refs_2_), channel_id=1, source_target_pairs={{0,1},{1,0},{2,3},{3,2},{4,5},{5,4},{6,7},{7,6},{8,9},{9,8},{10,11... | collective-permute-start | bytes 393224 | tf_op jit(solution)/shard_map/ppermute | solution.py:364
  21.8 6.0 %collective-permute-start.6 = (bf16[2,64,128]{2,1,0:T(8,128)(2,1)S(1)}, bf16[2,64,128]{2,1,0:T(8,128)(2,1)S(1)}, u32[]{:S(2)}, u32[]{:S(2)}) collective-permute-start(bf16[2,64,128]{2,1,0:T(8,128)(2,1)S(1)} %get-tuple-element.40), channel_id=1, source_target_pairs={{0,8},{4,12},{8,0},{12,4},{16,24},{20,28},{24,16},{28,20},{1,9},{5... | collective-permute-start | bytes 98312 | tf_op jit(solution)/shard_map/ppermute | solution.py:405
  23.7 5.4 %collective-permute-start.7 = (bf16[2,64,128]{2,1,0:T(8,128)(2,1)S(1)}, bf16[2,64,128]{2,1,0:T(8,128)(2,1)S(1)}, u32[]{:S(2)}, u32[]{:S(2)}) collective-permute-start(bf16[2,64,128]{2,1,0:T(8,128)(2,1)S(1)} %get-tuple-element.41), channel_id=1, source_target_pairs={{0,16},{4,20},{8,24},{12,28},{16,0},{20,4},{24,8},{28,12},{1,17},{... | collective-permute-start | bytes 98312 | tf_op jit(solution)/shard_map/ppermute | solution.py:405
  26.3 5.7 %collective-permute-start.8 = (bf16[2,64,128]{2,1,0:T(8,128)(2,1)S(1)}, bf16[2,64,128]{2,1,0:T(8,128)(2,1)S(1)}, u32[]{:S(2)}, u32[]{:S(2)}) collective-permute-start(bf16[2,64,128]{2,1,0:T(8,128)(2,1)S(1)} %get-tuple-element.42), channel_id=1, source_target_pairs={{0,24},{4,28},{8,16},{12,20},{16,8},{20,12},{24,0},{28,4},{1,25},{... | collective-permute-start | bytes 98312 | tf_op jit(solution)/shard_map/ppermute | solution.py:405
